TPU v7x, 32 devices: a whole 2x2x4 slice. The times are simulated.
32 devices in a mesh: dp: 8 (over z, y), space: 4 (over x, core).
Axes of the slice: x: 2, y: 2, z: 4, core: 2. Of those that a mesh axis runs over, the one named last changes fastest.
Arguments:
- volume: bfloat16 [8, 4, 32, 32, 32], P('dp', None, 'space'), may hold values from -6 to 6
- cotangent: bfloat16 [8, 64, 512], P('dp', None, 'space'), may hold values from -6 to 6
- conv_one: bfloat16 [32, 4, 3, 3, 3], replicated, may hold values from -0.625 to 0.625
- conv_two: bfloat16 [64, 32, 3, 3, 3], replicated, may hold values from -0.21875 to 0.21875
Outputs:
- out_two: bfloat16 [8, 64, 512], P('dp', None, 'space')
- grad_pre: bfloat16 [8, 32, 4096], P('dp', None, 'space')
- update_one: float32 [3456], replicated
- update_two: float32 [55296], replicated
All inputs are finite; a program needn't handle non-finite values.
Results may differ from a plain program's by a relative error of at most 0.0057.
Values may be sent and summed in bfloat16 or wider, within the bound.
A program may use at most 64 MiB of HBM per device.

v0:
```python
import jax
import jax.numpy as jnp
from jax import lax
from jax.sharding import PartitionSpec as P

damp_input = 0.1
damp_grad = 0.03


def passed_along(value, axis, steps):
    count = lax.axis_size(axis)
    leading, last = (max(0, -steps), min(count, count - steps))
    return lax.ppermute(value, axis, [(source, source + steps) for source in range(leading, last)])


def tap_stack(padded, out_depth, out_rows, out_cols):
    pieces = []
    for depth_tap in range(3):
        for row_tap in range(3):
            for col_tap in range(3):
                pieces.append(
                    padded[
                        :,
                        depth_tap : depth_tap + 2 * out_depth : 2,
                        row_tap : row_tap + 2 * out_rows : 2,
                        col_tap : col_tap + 2 * out_cols : 2,
                    ]
                )
    stacked = jnp.stack(pieces, axis=1)
    return stacked.reshape(stacked.shape[0] * 27, -1)


def spread_taps(columns, channels, out_depth, out_rows, out_cols):
    pieces = columns.reshape(channels, 27, out_depth, out_rows, out_cols)
    canvas = jnp.zeros(
        (channels, 2 * out_depth + 1, 2 * out_rows + 1, 2 * out_cols + 1), jnp.float32
    )
    for depth_tap in range(3):
        for row_tap in range(3):
            for col_tap in range(3):
                tap_number = depth_tap * 9 + row_tap * 3 + col_tap
                canvas = canvas.at[
                    :,
                    depth_tap : depth_tap + 2 * out_depth : 2,
                    row_tap : row_tap + 2 * out_rows : 2,
                    col_tap : col_tap + 2 * out_cols : 2,
                ].add(pieces[:, tap_number])
    return canvas


def silu_slope(pre_act):
    sigmoid_val = jax.nn.sigmoid(pre_act)
    return sigmoid_val * (1.0 + pre_act * (1.0 - sigmoid_val))


def damped_solve(matrix, rhs_terms):
    lower_factor = jnp.linalg.cholesky(matrix)
    return jax.scipy.linalg.cho_solve((lower_factor, True), rhs_terms)


def precondition(gram_in, gram_out, grad_sum, total_rows):
    in_mat = gram_in / total_rows + damp_input * jnp.eye(gram_in.shape[0], dtype=jnp.float32)
    out_mat = gram_out / total_rows + damp_grad * jnp.eye(gram_out.shape[0], dtype=jnp.float32)
    mean_grad = grad_sum / total_rows
    half_solved = damped_solve(in_mat, mean_grad.T).T
    return (damped_solve(out_mat, half_solved), mean_grad)


def on_device(volume, cotangent, conv_one, conv_two):
    local_volume = volume[0]
    cot_flat = cotangent[0]
    depth_len, row_count, col_count = (
        local_volume.shape[1],
        local_volume.shape[2],
        local_volume.shape[3],
    )
    width_one = conv_one.shape[0]
    width_two = conv_two.shape[0]
    weight_one = conv_one.reshape(width_one, -1)
    weight_two = conv_two.reshape(width_two, -1)
    lower_plane = passed_along(local_volume[:, depth_len - 1], "space", 1)
    extended = jnp.concatenate([lower_plane[:, None], local_volume], axis=1)
    padded = jnp.pad(extended, ((0, 0), (0, 0), (1, 0), (1, 0)))
    first_cols = tap_stack(padded, depth_len // 2, row_count // 2, col_count // 2)
    pre_one = jnp.dot(weight_one, first_cols, preferred_element_type=jnp.float32)
    act_one = (
        jax.nn.silu(pre_one)
        .astype(jnp.bfloat16)
        .reshape(width_one, depth_len // 2, row_count // 2, col_count // 2)
    )
    lower_act = passed_along(act_one[:, depth_len // 2 - 1], "space", 1)
    extended_two = jnp.concatenate([lower_act[:, None], act_one], axis=1)
    padded_two = jnp.pad(extended_two, ((0, 0), (0, 0), (1, 0), (1, 0)))
    second_cols = tap_stack(padded_two, depth_len // 4, row_count // 4, col_count // 4)
    out_two = jnp.dot(weight_two, second_cols, preferred_element_type=jnp.float32).astype(
        jnp.bfloat16
    )
    back_cols = jnp.dot(weight_two.T, cot_flat, preferred_element_type=jnp.float32)
    canvas = spread_taps(back_cols, width_one, depth_len // 4, row_count // 4, col_count // 4)
    grad_act = canvas[:, 1:, 1:, 1:]
    upper_part = passed_along(canvas[:, 0, 1:, 1:].astype(jnp.bfloat16), "space", -1).astype(
        jnp.float32
    )
    grad_act = grad_act.at[:, -1].add(upper_part)
    grad_pre = (grad_act.reshape(width_one, -1) * silu_slope(pre_one)).astype(jnp.bfloat16)
    in_one = jnp.dot(first_cols, first_cols.T, preferred_element_type=jnp.float32)
    gram_one = jnp.dot(grad_pre, grad_pre.T, preferred_element_type=jnp.float32)
    grad_one = jnp.dot(grad_pre, first_cols.T, preferred_element_type=jnp.float32)
    in_two = jnp.dot(second_cols, second_cols.T, preferred_element_type=jnp.float32)
    gram_two = jnp.dot(cot_flat, cot_flat.T, preferred_element_type=jnp.float32)
    grad_two = jnp.dot(cot_flat, second_cols.T, preferred_element_type=jnp.float32)
    summed = lax.psum((in_two, in_one, gram_one, grad_one, gram_two, grad_two), ("dp", "space"))
    total_in_two, total_in_one, total_gram_one, total_grad_one, total_gram_two, total_grad_two = (
        summed
    )
    device_count = lax.axis_size("dp") * lax.axis_size("space")
    rows_one = first_cols.shape[1] * device_count
    rows_two = cot_flat.shape[1] * device_count
    step_one, mean_one = precondition(total_in_one, total_gram_one, total_grad_one, rows_one)
    step_two, mean_two = precondition(total_in_two, total_gram_two, total_grad_two, rows_two)
    quad_form = jnp.sum(step_one * mean_one) + jnp.sum(step_two * mean_two)
    factor = jnp.sqrt((step_one.size + step_two.size) / quad_form)
    update_one = (factor * step_one).reshape(-1)
    update_two = (factor * step_two).reshape(-1)
    return (out_two[None], grad_pre[None], update_one, update_two)


def solution(mesh):
    in_specs = (P("dp", None, "space", None, None), P("dp", None, "space"), P(), P())
    out_specs = (P("dp", None, "space"), P("dp", None, "space"), P(), P())
    return jax.shard_map(
        on_device, mesh=mesh, in_specs=in_specs, out_specs=out_specs, check_vma=False
    )
```

profile of v0, /device:TPU:0, one launch (start us, length us, event | category | flops | bytes accessed | tf_op | source)
XLA Modules:
  0.0 933.9 jit_solution(1185647925688393770)
XLA Ops:
  12.8 8.7 scatter_fusion
  21.5 8.7 scatter_fusion.1
  30.3 8.6 scatter_fusion.2
  38.9 8.7 scatter_fusion.3
  47.6 8.7 scatter_fusion.4
  56.3 8.6 scatter_fusion.5
  65.0 8.7 scatter_fusion.6
  73.7 8.7 scatter_fusion.7
  82.4 8.6 scatter_fusion.8
  91.1 8.7 scatter_fusion.9
  99.8 8.7 scatter_fusion.10
  108.5 8.6 scatter_fusion.11
  117.1 8.9 scatter_fusion.12
  126.1 8.7 scatter_fusion.13
  134.8 8.6 scatter_fusion.14
  143.4 8.7 scatter_fusion.15
  152.2 8.7 scatter_fusion.16
  160.9 8.6 scatter_fusion.17
  169.5 8.7 scatter_fusion.18
  178.2 8.7 scatter_fusion.19
  187.0 8.6 scatter_fusion.20
  195.6 8.7 scatter_fusion.21
  204.3 8.7 scatter_fusion.22
  213.0 8.6 scatter_fusion.23
  221.7 9.1 scatter_fusion.24
  230.8 8.7 scatter_fusion.25
  239.6 8.6 scatter_fusion.26
  250.2 3.0 collective-permute-start
  255.5 5.7 slice.618
  261.2 5.7 slice.619
  266.9 5.7 slice.620
  272.5 5.7 slice.621
  278.2 5.6 slice.622
  283.8 5.7 slice.623
  289.5 5.7 slice.624
  356.0 4.0 copy.17
  363.0 4.5 collective-permute-start.1
  390.8 104.5 %all-reduce.10.cloned.1.call-done = (f32[108,108]{1,0:T(8,128)}, f32[32,108]{1,0:T(8,128)}, f32[32,32]{1,0:T(8,128)}, f32[64,64]{1,0:T(8,128)}) async-done(((f32[108,108]{1,0:T(8,128)}, f32[32,108]{1,0:T(8,128)}, f32[32,32]{1,0:T(8,128)}, f32[64,64]{1,0:T(8,128)}), (f32[108,108]{1,0:T(8,128)}, f32[32,108]{1,0:T(8,128)}, f32[32,32]{1,0:T(8,128)}, f32[64,64]{1,0:T(8,128)})) %all-reduce.10.cloned.1.call-update) | async-done | bytes 80976 | tf_op jit(solution)/shard_map/psum | solution.py:112
  497.0 9.9 %cholesky.246 = f32[108,108]{1,0:T(8,128)S(1)} custom-call(f32[108,108]{1,0:T(8,128)S(1)} %fusion.98), custom_call_target="Cholesky" | custom-call | tf_op jit(solution)/shard_map/jit(cholesky)/cholesky | solution.py:57
  509.8 2.9 cholesky.233
  514.8 8.3 custom-call.89
  523.1 2.4 custom-call.88
  526.4 5.8 cholesky.255
  533.6 5.5 custom-call.90
  542.7 97.4 %all-reduce.12.cloned.1.call-done = (f32[864,864]{1,0:T(8,128)}, f32[64,864]{1,0:T(8,128)}) async-done(((f32[864,864]{1,0:T(8,128)}, f32[64,864]{1,0:T(8,128)}), (f32[864,864]{1,0:T(8,128)}, f32[64,864]{1,0:T(8,128)})) %all-reduce.12.cloned.1.call-update) | async-done | bytes 3207184 | tf_op jit(solution)/shard_map/psum | solution.py:112
  640.1 3.8 select_add_fusion
  643.9 4.6 copy.28
  652.4 11.7 %cholesky.269 = f32[128,128]{1,0:T(8,128)S(1)} custom-call(f32[128,128]{1,0:T(8,128)S(1)} %cholesky.607), custom_call_target="Cholesky" | custom-call | tf_op jit(solution)/shard_map/jit(cholesky)/cholesky | solution.py:57
  665.1 9.8 %custom-call.91 = f32[1,128,128]{1,2,0:T(8,128)S(1)} custom-call(f32[1,128,128]{2,1,0:T(8,128)S(1)} %get-tuple-element.85), custom_call_target="InvertDiagBlocksLowerTriangular" | custom-call | tf_op jit(solution)/shard_map/jit(cholesky)/cholesky | solution.py:57
  678.4 12.5 %cholesky.492 = f32[128,128]{1,0:T(8,128)S(1)} custom-call(f32[128,128]{1,0:T(8,128)} %cholesky.611), custom_call_target="Cholesky" | custom-call | tf_op jit(solution)/shard_map/jit(cholesky)/cholesky | solution.py:57
  691.6 11.0 %custom-call.92 = f32[1,128,128]{1,2,0:T(8,128)S(1)} custom-call(f32[1,128,128]{2,1,0:T(8,128)} %get-tuple-element.82), custom_call_target="InvertDiagBlocksLowerTriangular" | custom-call | tf_op jit(solution)/shard_map/jit(cholesky)/cholesky | solution.py:57
  704.7 11.7 %cholesky.513 = f32[128,128]{1,0:T(8,128)S(1)} custom-call(f32[128,128]{1,0:T(8,128)S(1)} %cholesky.616), custom_call_target="Cholesky" | custom-call | tf_op jit(solution)/shard_map/jit(cholesky)/cholesky | solution.py:57
  716.5 9.8 %custom-call.93 = f32[1,128,128]{1,2,0:T(8,128)S(1)} custom-call(f32[1,128,128]{2,1,0:T(8,128)S(1)} %get-tuple-element.79), custom_call_target="InvertDiagBlocksLowerTriangular" | custom-call | tf_op jit(solution)/shard_map/jit(cholesky)/cholesky | solution.py:57
  728.3 11.9 %cholesky.532 = f32[128,128]{1,0:T(8,128)S(1)} custom-call(f32[128,128]{1,0:T(8,128)S(1)} %cholesky.621), custom_call_target="Cholesky" | custom-call | tf_op jit(solution)/shard_map/jit(cholesky)/cholesky | solution.py:57
  740.2 9.8 %custom-call.94 = f32[1,128,128]{1,2,0:T(8,128)S(1)} custom-call(f32[1,128,128]{2,1,0:T(8,128)S(1)} %get-tuple-element.76), custom_call_target="InvertDiagBlocksLowerTriangular" | custom-call | tf_op jit(solution)/shard_map/jit(cholesky)/cholesky | solution.py:57
  752.0 11.7 %cholesky.551 = f32[128,128]{1,0:T(8,128)S(1)} custom-call(f32[128,128]{1,0:T(8,128)S(1)} %cholesky.626), custom_call_target="Cholesky" | custom-call | tf_op jit(solution)/shard_map/jit(cholesky)/cholesky | solution.py:57
  763.8 9.8 %custom-call.95 = f32[1,128,128]{1,2,0:T(8,128)S(1)} custom-call(f32[1,128,128]{2,1,0:T(8,128)S(1)} %get-tuple-element.73), custom_call_target="InvertDiagBlocksLowerTriangular" | custom-call | tf_op jit(solution)/shard_map/jit(cholesky)/cholesky | solution.py:57
  775.4 11.9 %cholesky.571 = f32[128,128]{1,0:T(8,128)S(1)} custom-call(f32[128,128]{1,0:T(8,128)S(1)} %cholesky.631), custom_call_target="Cholesky" | custom-call | tf_op jit(solution)/shard_map/jit(cholesky)/cholesky | solution.py:57
  787.4 9.8 %custom-call.96 = f32[1,128,128]{1,2,0:T(8,128)S(1)} custom-call(f32[1,128,128]{2,1,0:T(8,128)S(1)} %get-tuple-element.70), custom_call_target="InvertDiagBlocksLowerTriangular" | custom-call | tf_op jit(solution)/shard_map/jit(cholesky)/cholesky | solution.py:57
  798.6 8.8 cholesky.592
  818.4 18.1 %while.2 = (s32[]{:T(128)}, f32[864,864]{1,0:T(8,128)}, s32[6,2]{0,1:T(2,128)S(1)}, f32[6,128,128]{2,1,0:T(8,128)S(1)}, s32[]{:T(128)}) while((s32[]{:T(128)}, f32[864,864]{1,0:T(8,128)}, s32[6,2]{0,1:T(2,128)S(1)}, f32[6,128,128]{2,1,0:T(8,128)S(1)}, s32[]{:T(128)}) %tuple.123), condition=%wide.while_cond.1, body=%wide.while_body.1.sunk | while | flops 2 | bytes 131189 | solution.py:58
  819.0 2.3 bitcast_dynamic-update-slice_fusion.2
  822.0 2.3 bitcast_dynamic-update-slice_fusion.2
  838.4 69.8 %custom-call.97 = f32[7,128,128]{1,2,0:T(8,128)S(1)} custom-call(f32[7,128,128]{2,1,0:T(8,128)} %pad_maximum_fusion), custom_call_target="InvertDiagBlocksLowerTriangular" | custom-call | tf_op jit(solution)/shard_map/jit(_cho_solve)/triangular_solve | solution.py:58
  (334 shorter events, 165.5 us)
Async XLA Ops:
  7.2 488.1 %all-reduce.10.cloned.1.call-start = ((), (), s32[]{:S(2)}) async-start(), calls=%async_computation | async-start | bytes 245760 | tf_op jit(solution)/shard_map/psum | solution.py:112
  239.5 10.6 %copy-start.8 = (bf16[1,4,8,32,32]{4,3,2,1,0:T(8,128)(2,1)S(1)}, bf16[1,4,8,32,32]{4,3,2,1,0:T(8,128)(2,1)}, u32[]{:S(2)}) copy-start(bf16[1,4,8,32,32]{4,3,2,1,0:T(8,128)(2,1)} %param.6) | copy-start | bytes 196612
  239.5 13.7 %copy-start.10 = (bf16[1,64,128]{2,1,0:T(8,128)(2,1)S(1)}, bf16[1,64,128]{2,1,0:T(8,128)(2,1)}, u32[]{:S(2)}) copy-start(bf16[1,64,128]{2,1,0:T(8,128)(2,1)} %param.7) | copy-start | bytes 49156
  239.5 15.7 %copy-start.12 = (bf16[32,4,3,3,3]{0,1,4,3,2:T(4,128)(2,1)S(1)}, bf16[32,4,3,3,3]{0,1,4,3,2:T(4,128)(2,1)}, u32[]{:S(2)}) copy-start(bf16[32,4,3,3,3]{0,1,4,3,2:T(4,128)(2,1)} %param.8) | copy-start | bytes 20740
  248.8 112.8 %collective-permute-start.2 = (bf16[32,16,16]{0,2,1:T(8,128)(2,1)}, bf16[32,16,16]{0,2,1:T(8,128)(2,1)}, u32[]{:S(2)}, u32[]{:S(2)}) collective-permute-start(bf16[32,16,16]{0,2,1:T(8,128)(2,1)} %fusion.66), channel_id=1, source_target_pairs={{1,0},{2,1},{3,2},{5,4},{6,5},{7,6},{9,8},{10,9},{11,10},{13,12},{... | collective-permute-start | bytes 49160 | tf_op jit(solution)/shard_map/ppermute | solution.py:13
  250.2 5.1 collective-permute-start
  362.8 20.5 %copy-start.4 = (bf16[32,1024]{1,0:T(8,128)(2,1)}, bf16[32,1024]{1,0:T(8,128)(2,1)S(1)}, u32[]{:S(2)}) copy-start(bf16[32,1024]{1,0:T(8,128)(2,1)S(1)} %get-tuple-element.67) | copy-start | bytes 196612
  363.0 6.1 collective-permute-start.1
  369.0 271.0 %all-reduce.12.cloned.1.call-start = ((), (), s32[]{:S(2)}) async-start(), calls=%async_computation.1 | async-start | bytes 6651904 | tf_op jit(solution)/shard_map/psum | solution.py:112
  643.9 4.6 copy-start
  650.8 1.6 copy-start.3
  652.4 12.0 %copy-start.5 = (f32[64,864]{1,0:T(8,128)S(1)}, f32[64,864]{1,0:T(8,128)}, u32[]{:S(2)}) copy-start(f32[64,864]{1,0:T(8,128)} %get-tuple-element.37) | copy-start | bytes 663556
  816.4 0.9 copy-start.13
  816.4 1.9 copy-start.7
  816.5 20.1 %copy-start.9 = (f32[128,32]{1,0:T(8,128)S(1)}, f32[128,32]{1,0:T(8,128)}, u32[]{:S(2)}) copy-start(f32[128,32]{1,0:T(8,128)} %pad_convert_fusion) | copy-start | bytes 49156
  816.7 1.7 copy-start.1
  836.5 78.4 %copy-start.2 = (f32[864,864]{1,0:T(8,128)S(1)}, f32[864,864]{1,0:T(8,128)}, u32[]{:S(2)}) copy-start(f32[864,864]{1,0:T(8,128)} %get-tuple-element.214) | copy-start | bytes 8957956
  913.3 8.2 copy-start.11
  914.9 7.1 copy-start.6
Sparse Core Ops, SparseCore 0:
  369.2 126.0 all-reduce.9
  500.9 139.1 all-reduce.11
where the time goes:
time: 946 us; the launch traced here: 934 us
  other arithmetic  507 us (54%)
  waiting for transfers between devices  202 us (21%)
  local copies, waits for them, and re-layouts  157 us (17%)
  matrix products  37.8 us (4%)
  between operations  22.1 us (2%)
    scatter-add x27, other arithmetic, spread_taps(): canvas = canvas.at[:, depth_tap:depth_tap + 2 * out_depth:2, row_tap:row_...  235 us
    psum x2, waiting for transfers between devices, on_device(): lax.psum((in_two, in_one, gram_one, grad_one, gram_two, grad_two), ('dp',...  202 us
    another operation x36, other arithmetic, damped_solve(): lower_factor = jnp.linalg.cholesky(matrix)  166 us
    another operation x13, other arithmetic, damped_solve(): return jax.scipy.linalg.cho_solve((lower_factor, True), rhs_terms)  91.3 us
    slice x54, local copies, waits for them, and re-layouts, tap_stack(): padded[:, depth_tap:depth_tap + 2 * out_depth:2, row_tap:row_tap + 2 * ou...  90.9 us
    unnamed x95, local copies, waits for them, and re-layouts  27 us
  transfers between devices with their start and end apart: 5, of which 2 were waited for; matrix products, arithmetic and copies ran while one was open for 19% of the time, Pallas kernels for 0%

commit v1 on v0

--- a/solution.py
+++ b/solution.py
@@ -109,7 +109,9 @@
     in_two = jnp.dot(second_cols, second_cols.T, preferred_element_type=jnp.float32)
     gram_two = jnp.dot(cot_flat, cot_flat.T, preferred_element_type=jnp.float32)
     grad_two = jnp.dot(cot_flat, second_cols.T, preferred_element_type=jnp.float32)
-    summed = lax.psum((in_two, in_one, gram_one, grad_one, gram_two, grad_two), ("dp", "space"))
+    summed = lax.psum(
+        lax.psum((in_two, in_one, gram_one, grad_one, gram_two, grad_two), "space"), "dp"
+    )
     total_in_two, total_in_one, total_gram_one, total_grad_one, total_gram_two, total_grad_two = (
         summed
     )

time: 946 us -> 999 us (1.056)
  waiting for transfers between devices: 202 us -> 255 us
    psum x2 -> x4, waiting for transfers between devices: 202 us -> 255 us  [the longest x2 168 us: on_device(): lax.psum(lax.psum((in_two, in_one, gram_one, grad_one, gram_two, grad_two...]
    unnamed x95 -> x101, local copies, waits for them, and re-layouts: 27 us -> 27.1 us
  transfers between devices with their start and end apart: 5 -> 7, of which waited for: 2 -> 4; matrix products, arithmetic and copies ran while one was open for 19% -> 17% of each run, Pallas kernels for 0% -> 0%
where the time goes in v1:
time: 999 us; the launch traced here: 987 us
  other arithmetic  507 us (51%)
  waiting for transfers between devices  255 us (26%)
  local copies, waits for them, and re-layouts  157 us (16%)
  matrix products  37.2 us (4%)
  between operations  21.6 us (2%)
    scatter-add x27, other arithmetic, spread_taps(): canvas = canvas.at[:, depth_tap:depth_tap + 2 * out_depth:2, row_tap:row_...  235 us
    another operation x36, other arithmetic, damped_solve(): lower_factor = jnp.linalg.cholesky(matrix)  171 us
    psum x2, waiting for transfers between devices, on_device(): lax.psum(lax.psum((in_two, in_one, gram_one, grad_one, gram_two, grad_two...  168 us
    slice x54, local copies, waits for them, and re-layouts, tap_stack(): padded[:, depth_tap:depth_tap + 2 * out_depth:2, row_tap:row_tap + 2 * ou...  91 us
    another operation x13, other arithmetic, damped_solve(): return jax.scipy.linalg.cho_solve((lower_factor, True), rhs_terms)  90.6 us
    psum x2, waiting for transfers between devices, on_device(): lax.psum((in_two, in_one, gram_one, grad_one, gram_two, grad_two), 'space')  86.8 us
    unnamed x101, local copies, waits for them, and re-layouts  27.1 us
  transfers between devices with their start and end apart: 7, of which 4 were waited for; matrix products, arithmetic and copies ran while one was open for 17% of the time, Pallas kernels for 0%

profile of v1, /device:TPU:0, one launch (start us, length us, event | category | flops | bytes accessed | tf_op | source)
XLA Modules:
  0.0 987.1 jit_solution(9919888693411945717)
XLA Ops:
  12.8 8.7 scatter_fusion
  21.5 8.7 scatter_fusion.1
  30.3 8.6 scatter_fusion.2
  38.9 8.7 scatter_fusion.3
  47.6 8.7 scatter_fusion.4
  56.3 8.6 scatter_fusion.5
  65.0 8.7 scatter_fusion.6
  73.7 8.7 scatter_fusion.7
  82.4 8.6 scatter_fusion.8
  91.1 8.7 scatter_fusion.9
  99.8 8.7 scatter_fusion.10
  108.5 8.6 scatter_fusion.11
  117.1 9.2 scatter_fusion.12
  126.3 8.7 scatter_fusion.13
  135.0 8.6 scatter_fusion.14
  143.7 8.7 scatter_fusion.15
  152.4 8.7 scatter_fusion.16
  161.1 8.6 scatter_fusion.17
  169.8 8.7 scatter_fusion.18
  178.5 8.7 scatter_fusion.19
  187.2 8.6 scatter_fusion.20
  195.9 8.7 scatter_fusion.21
  204.6 8.7 scatter_fusion.22
  213.3 8.6 scatter_fusion.23
  221.9 8.9 scatter_fusion.24
  230.8 8.7 scatter_fusion.25
  239.6 8.6 scatter_fusion.26
  250.2 3.0 collective-permute-start
  254.3 5.7 slice.618
  260.0 5.6 slice.619
  265.7 5.7 slice.620
  271.3 5.7 slice.621
  277.0 5.7 slice.622
  282.6 5.7 slice.623
  288.3 5.7 slice.624
  354.8 4.0 copy.17
  361.8 4.6 collective-permute-start.1
  387.8 13.8 %all-reduce.18.cloned.1.call-done = (f32[108,108]{1,0:T(8,128)}, f32[32,108]{1,0:T(8,128)}, f32[32,32]{1,0:T(8,128)}, f32[64,64]{1,0:T(8,128)}) async-done(((f32[108,108]{1,0:T(8,128)}, f32[32,108]{1,0:T(8,128)}, f32[32,32]{1,0:T(8,128)}, f32[64,64]{1,0:T(8,128)}), (f32[108,108]{1,0:T(8,128)}, f32[32,108]{1,0:T(8,128)}, f32[32,32]{1,0:T(8,128)}, f32[64,64]{1,0:T(8,128)})) %all-reduce.18.cloned.1.call-update) | async-done | bytes 80976 | tf_op jit(solution)/shard_map/psum | solution.py:113
  404.2 72.0 %all-reduce.14.cloned.1.call-done = (f32[108,108]{1,0:T(8,128)}, f32[32,108]{1,0:T(8,128)}, f32[32,32]{1,0:T(8,128)}, f32[64,64]{1,0:T(8,128)}) async-done(((f32[108,108]{1,0:T(8,128)}, f32[32,108]{1,0:T(8,128)}, f32[32,32]{1,0:T(8,128)}, f32[64,64]{1,0:T(8,128)}), (f32[108,108]{1,0:T(8,128)}, f32[32,108]{1,0:T(8,128)}, f32[32,32]{1,0:T(8,128)}, f32[64,64]{1,0:T(8,128)})) %all-reduce.14.cloned.1.call-update) | async-done | bytes 80976 | tf_op jit(solution)/shard_map/psum | solution.py:112
  477.3 73.0 %all-reduce.20.cloned.1.call-done = (f32[864,864]{1,0:T(8,128)}, f32[64,864]{1,0:T(8,128)}) async-done(((f32[864,864]{1,0:T(8,128)}, f32[64,864]{1,0:T(8,128)}), (f32[864,864]{1,0:T(8,128)}, f32[64,864]{1,0:T(8,128)})) %all-reduce.20.cloned.1.call-update) | async-done | bytes 3207184 | tf_op jit(solution)/shard_map/psum | solution.py:113
  550.3 9.9 %cholesky.246 = f32[108,108]{1,0:T(8,128)S(1)} custom-call(f32[108,108]{1,0:T(8,128)S(1)} %fusion.98), custom_call_target="Cholesky" | custom-call | tf_op jit(solution)/shard_map/jit(cholesky)/cholesky | solution.py:57
  561.5 8.3 custom-call.89
  569.9 2.9 cholesky.233
  574.2 2.4 custom-call.88
  576.8 5.8 cholesky.255
  583.9 5.5 custom-call.90
  591.6 96.1 %all-reduce.16.cloned.1.call-done = (f32[864,864]{1,0:T(8,128)}, f32[64,864]{1,0:T(8,128)}) async-done(((f32[864,864]{1,0:T(8,128)}, f32[64,864]{1,0:T(8,128)}), (f32[864,864]{1,0:T(8,128)}, f32[64,864]{1,0:T(8,128)})) %all-reduce.16.cloned.1.call-update) | async-done | bytes 3207184 | tf_op jit(solution)/shard_map/psum | solution.py:112
  687.7 3.8 select_add_fusion
  691.5 4.8 copy.28
  700.3 11.7 %cholesky.269 = f32[128,128]{1,0:T(8,128)S(1)} custom-call(f32[128,128]{1,0:T(8,128)S(1)} %cholesky.607), custom_call_target="Cholesky" | custom-call | tf_op jit(solution)/shard_map/jit(cholesky)/cholesky | solution.py:57
  712.9 9.8 custom-call.91
  726.3 13.2 %cholesky.492 = f32[128,128]{1,0:T(8,128)} custom-call(f32[128,128]{1,0:T(8,128)} %cholesky.611), custom_call_target="Cholesky" | custom-call | tf_op jit(solution)/shard_map/jit(cholesky)/cholesky | solution.py:57
  741.0 11.4 %custom-call.92 = f32[1,128,128]{1,2,0:T(8,128)} custom-call(f32[1,128,128]{2,1,0:T(8,128)} %get-tuple-element.88), custom_call_target="InvertDiagBlocksLowerTriangular" | custom-call | tf_op jit(solution)/shard_map/jit(cholesky)/cholesky | solution.py:57
  755.9 12.5 %cholesky.513 = f32[128,128]{1,0:T(8,128)S(1)} custom-call(f32[128,128]{1,0:T(8,128)} %cholesky.616), custom_call_target="Cholesky" | custom-call | tf_op jit(solution)/shard_map/jit(cholesky)/cholesky | solution.py:57
  769.1 10.6 %custom-call.93 = f32[1,128,128]{1,2,0:T(8,128)S(1)} custom-call(f32[1,128,128]{2,1,0:T(8,128)} %get-tuple-element.85), custom_call_target="InvertDiagBlocksLowerTriangular" | custom-call | tf_op jit(solution)/shard_map/jit(cholesky)/cholesky | solution.py:57
  781.8 11.9 %cholesky.532 = f32[128,128]{1,0:T(8,128)S(1)} custom-call(f32[128,128]{1,0:T(8,128)S(1)} %cholesky.621), custom_call_target="Cholesky" | custom-call | tf_op jit(solution)/shard_map/jit(cholesky)/cholesky | solution.py:57
  793.7 9.8 custom-call.94
  805.5 11.7 %cholesky.551 = f32[128,128]{1,0:T(8,128)S(1)} custom-call(f32[128,128]{1,0:T(8,128)S(1)} %cholesky.626), custom_call_target="Cholesky" | custom-call | tf_op jit(solution)/shard_map/jit(cholesky)/cholesky | solution.py:57
  817.3 9.8 custom-call.95
  828.9 12.1 %cholesky.571 = f32[128,128]{1,0:T(8,128)S(1)} custom-call(f32[128,128]{1,0:T(8,128)S(1)} %cholesky.631), custom_call_target="Cholesky" | custom-call | tf_op jit(solution)/shard_map/jit(cholesky)/cholesky | solution.py:57
  841.0 9.8 custom-call.96
  852.3 8.8 cholesky.592
  872.0 18.3 %while.2 = (s32[]{:T(128)}, f32[864,864]{1,0:T(8,128)}, s32[6,2]{0,1:T(2,128)S(1)}, f32[6,128,128]{2,1,0:T(8,128)S(1)}, s32[]{:T(128)}) while((s32[]{:T(128)}, f32[864,864]{1,0:T(8,128)}, s32[6,2]{0,1:T(2,128)S(1)}, f32[6,128,128]{2,1,0:T(8,128)S(1)}, s32[]{:T(128)}) %tuple.129), condition=%wide.while_cond.1, body=%wide.while_body.1.sunk | while | flops 2 | bytes 131189 | solution.py:58
  892.2 69.7 %custom-call.97 = f32[7,128,128]{1,2,0:T(8,128)S(1)} custom-call(f32[7,128,128]{2,1,0:T(8,128)} %pad_maximum_fusion), custom_call_target="InvertDiagBlocksLowerTriangular" | custom-call | tf_op jit(solution)/shard_map/jit(_cho_solve)/triangular_solve | solution.py:58
  (346 shorter events, 167.6 us)
Async XLA Ops:
  7.2 394.5 %all-reduce.18.cloned.1.call-start = ((), (), s32[]{:S(2)}) async-start(), calls=%async_computation.2 | async-start | bytes 245760 | tf_op jit(solution)/shard_map/psum | solution.py:113
  239.5 10.6 %copy-start.8 = (bf16[1,4,8,32,32]{4,3,2,1,0:T(8,128)(2,1)S(1)}, bf16[1,4,8,32,32]{4,3,2,1,0:T(8,128)(2,1)}, u32[]{:S(2)}) copy-start(bf16[1,4,8,32,32]{4,3,2,1,0:T(8,128)(2,1)} %param.6) | copy-start | bytes 196612
  239.6 13.7 %copy-start.10 = (bf16[1,64,128]{2,1,0:T(8,128)(2,1)S(1)}, bf16[1,64,128]{2,1,0:T(8,128)(2,1)}, u32[]{:S(2)}) copy-start(bf16[1,64,128]{2,1,0:T(8,128)(2,1)} %param.7) | copy-start | bytes 49156
  239.6 14.5 %copy-start.15 = (bf16[32,4,3,3,3]{0,1,4,3,2:T(4,128)(2,1)S(1)}, bf16[32,4,3,3,3]{0,1,4,3,2:T(4,128)(2,1)}, u32[]{:S(2)}) copy-start(bf16[32,4,3,3,3]{0,1,4,3,2:T(4,128)(2,1)} %param.8) | copy-start | bytes 20740
  248.9 111.6 %collective-permute-start.2 = (bf16[32,16,16]{0,2,1:T(8,128)(2,1)}, bf16[32,16,16]{0,2,1:T(8,128)(2,1)}, u32[]{:S(2)}, u32[]{:S(2)}) collective-permute-start(bf16[32,16,16]{0,2,1:T(8,128)(2,1)} %fusion.66), channel_id=1, source_target_pairs={{1,0},{2,1},{3,2},{5,4},{6,5},{7,6},{9,8},{10,9},{11,10},{13,12},{... | collective-permute-start | bytes 49160 | tf_op jit(solution)/shard_map/ppermute | solution.py:13
  250.2 3.9 collective-permute-start
  361.6 20.6 %copy-start.4 = (bf16[32,1024]{1,0:T(8,128)(2,1)}, bf16[32,1024]{1,0:T(8,128)(2,1)S(1)}, u32[]{:S(2)}) copy-start(bf16[32,1024]{1,0:T(8,128)(2,1)S(1)} %get-tuple-element.73) | copy-start | bytes 196612
  361.8 6.2 collective-permute-start.1
  368.0 108.3 %all-reduce.14.cloned.1.call-start = ((), (), s32[]{:S(2)}) async-start(), calls=%async_computation | async-start | bytes 245760 | tf_op jit(solution)/shard_map/psum | solution.py:112
  401.6 148.6 %all-reduce.20.cloned.1.call-start = ((), (), s32[]{:S(2)}) async-start(), calls=%async_computation.3 | async-start | bytes 6651904 | tf_op jit(solution)/shard_map/psum | solution.py:113
  402.6 285.1 %all-reduce.16.cloned.1.call-start = ((), (), s32[]{:S(2)}) async-start(), calls=%async_computation.1 | async-start | bytes 6651904 | tf_op jit(solution)/shard_map/psum | solution.py:112
  476.3 74.0 %copy-start.9 = (f32[108,108]{1,0:T(8,128)S(1)}, f32[108,108]{1,0:T(8,128)}, u32[]{:S(2)}) copy-start(f32[108,108]{1,0:T(8,128)} %get-tuple-element.32) | copy-start | bytes 139972
  476.3 93.6 %copy-start.13 = (f32[32,32]{1,0:T(8,128)S(1)}, f32[32,32]{1,0:T(8,128)}, u32[]{:S(2)}) copy-start(f32[32,32]{1,0:T(8,128)} %get-tuple-element.34) | copy-start | bytes 12292
  476.3 100.3 %copy-start.11 = (f32[64,64]{1,0:T(8,128)S(1)}, f32[64,64]{1,0:T(8,128)}, u32[]{:S(2)}) copy-start(f32[64,64]{1,0:T(8,128)} %get-tuple-element.35) | copy-start | bytes 49156
  476.3 113.2 %copy-start.14 = (f32[32,108]{1,0:T(8,128)S(1)}, f32[32,108]{1,0:T(8,128)}, u32[]{:S(2)}) copy-start(f32[32,108]{1,0:T(8,128)} %get-tuple-element.33) | copy-start | bytes 41476
  691.5 4.8 copy-start
  698.6 1.6 copy-start.3
  700.2 12.0 %copy-start.5 = (f32[64,864]{1,0:T(8,128)S(1)}, f32[64,864]{1,0:T(8,128)}, u32[]{:S(2)}) copy-start(f32[64,864]{1,0:T(8,128)} %get-tuple-element.37) | copy-start | bytes 663556
  870.1 0.9 copy-start.16
  870.1 1.9 copy-start.7
  870.4 1.7 copy-start.1
  890.3 78.3 %copy-start.2 = (f32[864,864]{1,0:T(8,128)S(1)}, f32[864,864]{1,0:T(8,128)}, u32[]{:S(2)}) copy-start(f32[864,864]{1,0:T(8,128)} %get-tuple-element.232) | copy-start | bytes 8957956
  967.1 8.2 copy-start.12
  968.6 7.1 copy-start.6
Sparse Core Ops, SparseCore 0:
  368.1 33.4 all-reduce.17
  405.3 70.9 all-reduce.13
  478.7 71.4 all-reduce.19
  553.8 133.8 all-reduce.15
